TPU v7x, 32 devices: a whole 2x2x4 slice. The times are simulated.
32 devices in a mesh: rep: 2 (over x), fsdp: 4 (over z), ctx: 4 (over y, core).
Axes of the slice: x: 2, y: 2, z: 4, core: 2. Of those that a mesh axis runs over, the one named last changes fastest.
Arguments:
- inputs: bfloat16 [8, 1024, 2048], P(('rep', 'fsdp'), 'ctx'), may hold values from -6 to 6
- prefix: int32 [8], P(('rep', 'fsdp')), may hold values from 102 to 512
- joined_weight: bfloat16 [2048, 6144], P(('fsdp', 'ctx')), may hold values from -0.125 to 0.125
- query_bias: bfloat16 [2048], P(('fsdp', 'ctx')), may hold values from -3 to 3
- value_bias: bfloat16 [2048], P(('fsdp', 'ctx')), may hold values from -3 to 3
- dense_weight: bfloat16 [2048, 2048], P(('fsdp', 'ctx')), may hold values from -0.5 to 0.5
- dense_bias: bfloat16 [2048], P(('fsdp', 'ctx')), may hold values from -2 to 2
- expand_weight: bfloat16 [2048, 8192], P(('fsdp', 'ctx')), may hold values from -0.125 to 0.125
- expand_bias: bfloat16 [8192], P(('fsdp', 'ctx')), may hold values from -3 to 3
- shrink_weight: bfloat16 [8192, 2048], P(('fsdp', 'ctx')), may hold values from -0.0625 to 0.0625
- shrink_bias: bfloat16 [2048], P(('fsdp', 'ctx')), may hold values from -2 to 2
- first_gain: bfloat16 [2048], P(('fsdp', 'ctx')), may hold values from 0.5 to 1.5
- first_shift: bfloat16 [2048], P(('fsdp', 'ctx')), may hold values from -2 to 2
- second_gain: bfloat16 [2048], P(('fsdp', 'ctx')), may hold values from 0.5 to 1.5
- second_shift: bfloat16 [2048], P(('fsdp', 'ctx')), may hold values from -2 to 2
- cotangent: bfloat16 [8, 1024, 2048], P(('rep', 'fsdp'), 'ctx'), may hold values from -6 to 6
Outputs:
- layer_output: float32 [8, 1024, 2048], P(('rep', 'fsdp'), 'ctx')
- input_gradient: float32 [8, 1024, 2048], P(('rep', 'fsdp'), 'ctx')
- joined_gradient: float32 [2048, 6144], P(('fsdp', 'ctx'))
- query_bias_gradient: float32 [2048], P(('fsdp', 'ctx'))
- value_bias_gradient: float32 [2048], P(('fsdp', 'ctx'))
- dense_gradient: float32 [2048, 2048], P(('fsdp', 'ctx'))
- dense_bias_gradient: float32 [2048], P(('fsdp', 'ctx'))
- expand_gradient: float32 [2048, 8192], P(('fsdp', 'ctx'))
- expand_bias_gradient: float32 [8192], P(('fsdp', 'ctx'))
- shrink_gradient: float32 [8192, 2048], P(('fsdp', 'ctx'))
- shrink_bias_gradient: float32 [2048], P(('fsdp', 'ctx'))
- first_gain_gradient: float32 [2048], P(('fsdp', 'ctx'))
- first_shift_gradient: float32 [2048], P(('fsdp', 'ctx'))
- second_gain_gradient: float32 [2048], P(('fsdp', 'ctx'))
- second_shift_gradient: float32 [2048], P(('fsdp', 'ctx'))
All inputs are finite; a program needn't handle non-finite values.
Results may differ from a plain program's by a relative error of at most 0.014.
Values may be sent and summed in bfloat16 or wider, within the bound.
No kernel may reach another device: no remote copies, remote signals or barrier semaphores. Data moves between devices by JAX's collectives and lax.ppermute only.
A program may use at most 576 MiB of HBM per device.

v0:
```python
import jax
import jax.numpy as jnp
from jax import lax
from jax.sharding import PartitionSpec as P

H = 32
HD = 64
TP = ("rep", "ctx")
BF = jnp.bfloat16
F32 = jnp.float32


def dot(a, b, ca, cb):
    return lax.dot_general(a, b, (((ca,), (cb,)), ((), ())), preferred_element_type=F32)


def norm_stats(values):
    average = jnp.mean(values, axis=-1, keepdims=True)
    centred = values - average
    variance = jnp.mean(centred * centred, axis=-1, keepdims=True)
    inverse = lax.rsqrt(variance + 1e-05)
    return (centred * inverse, inverse)


def norm_back(normed, inverse, gain, grad):
    u = grad * gain
    mean_u = jnp.mean(u, axis=-1, keepdims=True)
    mean_un = jnp.mean(u * normed, axis=-1, keepdims=True)
    return (u - mean_u - normed * mean_un) * inverse


def gelu(values):
    return 0.5 * values * (1.0 + lax.erf(values * 0.7071067811865476))


def gelu_slope(values):
    density = jnp.exp(values * values * -0.5) * 0.3989422804014327
    return 0.5 * (1.0 + lax.erf(values * 0.7071067811865476)) + values * density


def gather_tp(x):
    return lax.all_gather(x, TP, axis=0, tiled=True)


def scatter_tp(x):
    return lax.psum_scatter(x, TP, scatter_dimension=0, tiled=True)


def swap_tp(x):
    return lax.all_to_all(x, TP, 0, 0, tiled=True)


def attention_logits(q, k, heads, prefix):
    raw = jnp.einsum("sqhe,skhe->shqk", q, k, preferred_element_type=F32)
    length = k.shape[1]
    place = jnp.arange(length, dtype=jnp.int32)
    distance = jnp.abs(place[:, None] - place[None, :]).astype(F32)
    allowed = (place[None, None, :] <= place[None, :, None]) | (
        place[None, None, :] < prefix[:, None, None]
    )
    slopes = jnp.exp2(-8.0 * (heads.astype(F32) + 1.0) / H)
    logits = raw * 0.125 - slopes[None, :, None, None] * distance[None, None]
    return (logits, allowed[:, None])


def attention_forward(q, k, v, heads, prefix):
    logits, allowed = attention_logits(q, k, heads, prefix)
    masked = jnp.where(allowed, logits, -1e30)
    largest = jnp.max(masked, axis=-1, keepdims=True)
    exponent = jnp.exp(masked - largest)
    totals = jnp.sum(exponent, axis=-1, keepdims=True)
    probs = (exponent / totals).astype(BF)
    out = jnp.einsum("shqk,skhe->sqhe", probs, v, preferred_element_type=F32).astype(BF)
    return (out, largest + jnp.log(totals))


def attention_backward(q, k, v, lse, d_out, heads, prefix):
    logits, allowed = attention_logits(q, k, heads, prefix)
    probs = jnp.where(allowed, jnp.exp(logits - lse), 0.0)
    d_probs = jnp.einsum("sqhe,skhe->shqk", d_out, v, preferred_element_type=F32)
    weighted = jnp.sum(probs * d_probs, axis=-1, keepdims=True)
    d_raw = (probs * (d_probs - weighted) * 0.125).astype(BF)
    low = probs.astype(BF)
    d_q = jnp.einsum("shqk,skhe->sqhe", d_raw, k, preferred_element_type=F32).astype(BF)
    d_k = jnp.einsum("shqk,sqhe->skhe", d_raw, q, preferred_element_type=F32).astype(BF)
    d_v = jnp.einsum("shqk,sqhe->skhe", low, d_out, preferred_element_type=F32).astype(BF)
    return (d_q, d_k, d_v)


def shards(
    sizes,
    inputs,
    prefix,
    joined_weight,
    query_bias,
    value_bias,
    dense_weight,
    dense_bias,
    expand_weight,
    expand_bias,
    shrink_weight,
    shrink_bias,
    first_gain,
    first_shift,
    second_gain,
    second_shift,
    cotangent,
):
    R, F, C = sizes
    N = R * C
    rep = lax.axis_index("rep")
    ctx = lax.axis_index("ctx")
    S, T, D = inputs.shape
    t = S * T
    B = joined_weight.shape[0]
    FFB = shrink_weight.shape[0]
    FF = FFB * F * C
    E = FFB // R
    W = D // N
    aligned = B // R % HD == 0

    def split_columns(weight, groups):
        n = weight.shape[1] // groups
        if aligned or groups == 1:
            pieces = weight.reshape(B, groups, F, C, R, n // (F * C * R))
            mine = lax.dynamic_index_in_dim(pieces, rep, 4, keepdims=False)
            mine = mine.transpose(3, 0, 1, 2, 4)
        else:
            pieces = weight.reshape(B, groups, R, C, n // (C * R))
            mine = lax.dynamic_index_in_dim(pieces, rep, 2, keepdims=False)
            mine = mine.transpose(2, 0, 1, 3)
        return mine.reshape(C, B, groups * n // N)

    def columns(weight, groups):
        blocks = lax.all_to_all(split_columns(weight, groups), "ctx", 0, 0, tiled=True)
        return lax.all_gather(blocks.reshape(C * B, -1), "fsdp", axis=0, tiled=True)

    def join_columns(grad, groups):
        part = lax.psum_scatter(grad.astype(BF), "fsdp", scatter_dimension=0, tiled=True)
        blocks = lax.all_to_all(part.reshape(C, B, -1), "ctx", 0, 0, tiled=True)
        both = lax.all_gather(blocks, "rep", axis=0, tiled=False)
        if aligned or groups == 1:
            both = both.reshape(R, C, B, groups, F, -1).transpose(2, 3, 4, 1, 0, 5)
        else:
            both = both.reshape(R, C, B, groups, -1).transpose(2, 3, 0, 1, 4)
        return both.reshape(B, -1).astype(F32)

    def half_rows(weight):
        n = weight.shape[0] // R
        return lax.dynamic_slice_in_dim(weight, rep * n, n, 0)

    def join_rows(part):
        return lax.all_gather(part, "rep", axis=0, tiled=True).astype(F32)

    small = jnp.concatenate(
        [
            first_gain,
            first_shift,
            second_gain,
            second_shift,
            dense_bias,
            shrink_bias,
            query_bias,
            value_bias,
            expand_bias,
        ]
    )
    small = lax.all_gather(small, ("fsdp", "ctx"), axis=0, tiled=False).astype(F32)
    gain_one, shift_one, gain_two, shift_two, dbias, sbias, qbias, vbias = [
        small[:, i * B : (i + 1) * B].reshape(D) for i in range(8)
    ]
    ebias = small[:, 8 * B :].reshape(F, C, R, E)
    ebias = lax.dynamic_index_in_dim(
        lax.dynamic_index_in_dim(ebias, ctx, 1, False), rep, 1, False
    ).reshape(F * E)

    def my_features(vector):
        if aligned:
            v = vector.reshape(F, C, R, -1)
            return lax.dynamic_index_in_dim(
                lax.dynamic_index_in_dim(v, ctx, 1, False), rep, 1, False
            ).reshape(W)
        return lax.dynamic_slice_in_dim(vector, (rep * C + ctx) * W, W, 0)

    my_heads = my_features(jnp.repeat(jnp.arange(H, dtype=jnp.int32), HD)).reshape(-1, HD)[:, 0]
    prefix_all = lax.all_gather(prefix, "rep", axis=0, tiled=True)
    joined_cols = columns(joined_weight, 3)
    dense_rows = (
        lax.all_gather(half_rows(dense_weight), "fsdp", axis=0, tiled=True) if aligned else None
    )
    expand_cols = columns(expand_weight, 1)
    shrink_rows = lax.all_gather(half_rows(shrink_weight), "fsdp", axis=0, tiled=True)
    if aligned:
        dense_all = gather_tp(dense_rows)
    else:
        dense_all = lax.all_gather(dense_weight, ("fsdp", "ctx"), axis=0, tiled=True)

    def to_sequences(a):
        return a.reshape(R, C, S, T, -1).transpose(0, 2, 1, 3, 4).reshape(R * S, C * T, -1)

    def from_sequences(a):
        return a.reshape(R, S, C, T, -1).transpose(0, 2, 1, 3, 4).reshape(N * t, -1)

    start = inputs.astype(F32).reshape(t, D)
    n1, inv1 = norm_stats(start)
    a1 = (n1 * gain_one + shift_one).astype(BF)
    a1_all = gather_tp(a1)
    g = cotangent.reshape(t, D)
    g_all = gather_tp(g)
    qkv = dot(a1_all, joined_cols, 1, 0)
    q = (qkv[:, :W] + my_features(qbias)).astype(BF)
    k = qkv[:, W : 2 * W].astype(BF)
    v = (qkv[:, 2 * W :] + my_features(vbias)).astype(BF)
    heads = lambda a: to_sequences(a).reshape(R * S, C * T, W // HD, HD)
    q, k, v = (heads(q), heads(k), heads(v))
    out, lse = attention_forward(q, k, v, my_heads, prefix_all)
    o = swap_tp(from_sequences(out).reshape(N, t, W))
    o = o.transpose(1, 0, 2).reshape(t, D)
    midway = start + dot(o, dense_all, 1, 0) + dbias
    n2, inv2 = norm_stats(midway)
    a2 = (n2 * gain_two + shift_two).astype(BF)
    a2_all = gather_tp(a2)
    expanded = dot(a2_all, expand_cols, 1, 0) + ebias
    act = gelu(expanded).astype(BF)
    branch = scatter_tp(dot(act, shrink_rows, 1, 0).astype(BF))
    layer_output = midway + branch.astype(F32) + sbias
    g_float = g.astype(F32)
    d_act = dot(g_all, shrink_rows, 1, 1)
    d_exp = (d_act * gelu_slope(expanded)).astype(BF)
    d_a2 = scatter_tp(dot(d_exp, expand_cols, 1, 1).astype(BF)).astype(F32)
    shrink_grad = dot(act, g_all, 0, 0).astype(BF)
    expand_grad = dot(a2_all, d_exp, 0, 0)
    ebias_grad = jnp.sum(d_exp.astype(F32), axis=0)
    sbias_grad = jnp.sum(g_float, axis=0)
    d_mid = g_float + norm_back(n2, inv2, gain_two, d_a2)
    gain_two_grad = jnp.sum(d_a2 * n2, axis=0)
    shift_two_grad = jnp.sum(d_a2, axis=0)
    d_att = d_mid.astype(BF)
    dense_grad = dot(o, d_att, 0, 0)
    dbias_grad = jnp.sum(d_att.astype(F32), axis=0)
    d_o = dot(d_att, dense_all, 1, 1).astype(BF)
    d_o = swap_tp(d_o.reshape(t, N, W).transpose(1, 0, 2)).reshape(N * t, W)
    d_q, d_k, d_v = attention_backward(q, k, v, lse, heads(d_o), my_heads, prefix_all)
    d_qkv = jnp.concatenate(
        [from_sequences(a.reshape(R * S, C * T, W)) for a in (d_q, d_k, d_v)], axis=1
    )
    d_a1 = scatter_tp(dot(d_qkv, joined_cols, 1, 1).astype(BF)).astype(F32)
    joined_grad = dot(a1_all, d_qkv, 0, 0)
    qkv_bias_grad = jnp.sum(d_qkv.astype(F32), axis=0)
    input_gradient = d_mid + norm_back(n1, inv1, gain_one, d_a1)
    gain_one_grad = jnp.sum(d_a1 * n1, axis=0)
    shift_one_grad = jnp.sum(d_a1, axis=0)
    shrink_out = join_rows(lax.psum_scatter(shrink_grad, "fsdp", scatter_dimension=0, tiled=True))
    expand_out = join_columns(expand_grad, 1)
    if aligned:
        part = scatter_tp(dense_grad.astype(BF))
        dense_out = join_rows(lax.psum_scatter(part, "fsdp", scatter_dimension=0, tiled=True))
    else:
        part = lax.psum_scatter(
            dense_grad.astype(BF), ("fsdp", "ctx"), scatter_dimension=0, tiled=True
        )
        dense_out = lax.psum(part, "rep").astype(F32)
    joined_out = join_columns(joined_grad, 3)

    def spread(vector, width):
        if aligned or width != D:
            full = jnp.zeros((F, C, R, width // (F * C * R)), F32)
            full = lax.dynamic_update_slice(full, vector.reshape(F, 1, 1, -1), (0, ctx, rep, 0))
        else:
            full = lax.dynamic_update_slice_in_dim(
                jnp.zeros((width,), F32), vector, (rep * C + ctx) * W, 0
            )
        return full.reshape(F * C, -1)

    tokens = [gain_one_grad, shift_one_grad, gain_two_grad, shift_two_grad, dbias_grad, sbias_grad]
    rows = [a.reshape(F * C, B) for a in tokens]
    rows += [
        spread(qkv_bias_grad[:W], D),
        spread(qkv_bias_grad[2 * W :], D),
        spread(ebias_grad, FF),
    ]
    little = jnp.concatenate(rows, axis=1)
    little = lax.psum(
        lax.psum_scatter(little, ("fsdp", "ctx"), scatter_dimension=0, tiled=True), "rep"
    ).reshape(-1)
    (
        gain_one_out,
        shift_one_out,
        gain_two_out,
        shift_two_out,
        dbias_out,
        sbias_out,
        qbias_out,
        vbias_out,
    ) = [little[i * B : (i + 1) * B] for i in range(8)]
    ebias_out = little[8 * B :]
    return (
        layer_output.reshape(S, T, D),
        input_gradient.reshape(S, T, D),
        joined_out,
        qbias_out,
        vbias_out,
        dense_out,
        dbias_out,
        expand_out,
        ebias_out,
        shrink_out,
        sbias_out,
        gain_one_out,
        shift_one_out,
        gain_two_out,
        shift_two_out,
    )


def solution(mesh):
    sizes = (mesh.shape["rep"], mesh.shape["fsdp"], mesh.shape["ctx"])
    tokens = P(("rep", "fsdp"), "ctx", None)
    matrix = P(("fsdp", "ctx"), None)
    vector = P(("fsdp", "ctx"))
    in_specs = (
        tokens,
        P(("rep", "fsdp")),
        matrix,
        vector,
        vector,
        matrix,
        vector,
        matrix,
        vector,
        matrix,
        vector,
        vector,
        vector,
        vector,
        vector,
        tokens,
    )
    out_specs = (
        tokens,
        tokens,
        matrix,
        vector,
        vector,
        matrix,
        vector,
        matrix,
        vector,
        matrix,
        vector,
        vector,
        vector,
        vector,
        vector,
    )

    def step(*arrays):
        return shards(sizes, *arrays)

    return jax.shard_map(step, mesh=mesh, in_specs=in_specs, out_specs=out_specs, check_vma=False)
```

profile of v0, /device:TPU:0, one launch (start us, length us, event | category | flops | bytes accessed | tf_op | source)
XLA Modules:
  0.0 1312.8 jit_solution(1803940489215172898)
XLA Ops:
  13.2 15.8 %all_to_all.30 = bf16[4,128,768]{1,2,0:T(8,128)(2,1)} all-to-all(bf16[4,128,768]{1,2,0:T(8,128)(2,1)S(1)} %bitcast.219), channel_id=1, replica_groups=mesh['rep'=2,'fsdp'=4,'ctx'=4] {'ctx'}, dimensions={0} | all-to-all | bytes 1572864 | tf_op jit(solution)/shard_map/all_to_all | solution.py:135
  33.2 21.2 %all-gather.4 = bf16[16,1,1536]{2,1,0:T(2,128)(2,1)S(1)} all-gather(bf16[1,1,1536]{2,1,0:T(2,128)(2,1)S(1)} %reshape.335), channel_id=2, replica_groups=mesh['rep'=2,'fsdp'=4,'ctx'=4] {'fsdp','ctx'}, dimensions={0}, use_global_device_ids=true | all-gather | bytes 52224 | tf_op jit(solution)/shard_map/all_gather | solution.py:168
  76.2 8.1 broadcast_multiply_fusion
  96.1 10.1 all-gather.19.cloned.1.call-done
  106.2 55.5 %all-gather.17.cloned.1.call-done = bf16[2048,2048]{1,0:T(8,128)(2,1)} async-done(((bf16[256,2048]{1,0:T(8,128)(2,1)}), bf16[2048,2048]{1,0:T(8,128)(2,1)}) %all-gather.17.cloned.1.call-update) | async-done | bytes 8388624 | tf_op jit(solution)/shard_map/all_gather | solution.py:42
  161.7 10.0 fusion.93
  191.5 4.5 reshape.342
  200.1 22.8 %select_reduce_fusion = (f32[2,4,1024]{2,1,0:T(4,128)S(1)}, f32[2,4,1024,1024]{2,3,1,0:T(8,128)}) fusion(f32[4,1024,1024]{1,2,0:T(8,128)} %broadcast_multiply_fusion, pred[2,1024,1024]{1,2,0:T(8,128)(4,1)} %broadcast_or_fusion, bf16[2,1024,4,64]{1,3,2,0:T(8,128)(2,1)} %copy.112, bf16[2,1024,4,64]{1,3,2,0:T(8,128)(2,1)} %copy.113), kind=kOutput, calls=%fused_computation.8 | convolution fusion | flops 1107288064 | bytes 54558720 | tf_op jit(solution)/shard_map/sqhe,skhe->shqk/dot_general | solution.py:54
  222.9 19.0 %fusion.4 = f32[2,4,1024]{2,1,0:T(4,128)S(1)} fusion(f32[2,4,1024,1024]{2,3,1,0:T(8,128)} %get-tuple-element.92, f32[2,4,1024]{2,1,0:T(4,128)S(1)} %get-tuple-element.91, f32[4,1024,1024]{1,2,0:T(8,128)} %broadcast_multiply_fusion, pred[2,1024,1024]{1,2,0:T(8,128)(4,1)S(1)} %copy-done.2), kind=kLoop, calls=%fused_computation.9 | loop fusion | flops 41934848 | bytes 52494336 | tf_op jit(solution)/shard_map/reduce_sum | solution.py:71
  241.9 19.5 %fusion.72 = bf16[2,1024,4,64]{1,3,2,0:T(8,128)(2,1)S(1)} fusion(bf16[2,1024,4,64]{1,3,2,0:T(8,128)(2,1)S(1)} %copy-done.13, f32[2,4,1024,1024]{2,3,1,0:T(8,128)} %get-tuple-element.92, f32[2,4,1024]{2,1,0:T(4,128)S(1)} %fusion.4, f32[2,4,1024]{2,1,0:T(4,128)S(1)} %get-tuple-element.91, f32[4,1024,1024]{1,2,0:T(8,128)} %broadcast_multiply_fusion, ...), kind=kOutput, calls=%fused_computation.92 | convolution fusion | flops 1124597760 | bytes 54591488 | tf_op jit(solution)/shard_map/shqk,skhe->sqhe/dot_general | solution.py:73
  267.1 17.7 %all_to_all.31 = bf16[8,256,256]{1,2,0:T(8,128)(2,1)} all-to-all(bf16[8,256,256]{1,2,0:T(8,128)(2,1)S(1)} %copy.117), channel_id=1, replica_groups=mesh['rep'=2,'fsdp'=4,'ctx'=4] {'rep','ctx'}, dimensions={0} | all-to-all | bytes 2097152 | tf_op jit(solution)/shard_map/all_to_all | solution.py:50
  284.8 6.2 fusion.92
  295.8 4.8 all-gather.27.cloned.1.call-done
  300.7 55.3 %all-gather.25.cloned.1.call-done = bf16[2048,2048]{1,0:T(8,128)(2,1)} async-done(((bf16[256,2048]{1,0:T(8,128)(2,1)}), bf16[2048,2048]{1,0:T(8,128)(2,1)}) %all-gather.25.cloned.1.call-update) | async-done | bytes 8388624 | tf_op jit(solution)/shard_map/all_gather | solution.py:42
  355.9 15.9 %multiply_convert_fusion.1 = (bf16[2048,1024]{1,0:T(8,128)(2,1)}, f32[2048,1024]{1,0:T(8,128)}) fusion(f32[1024]{0:T(1024)S(1)} %bitcast.232, bf16[2048,2048]{1,0:T(8,128)(2,1)} %all-gather.25.cloned.1.call-done, bf16[2048,1024]{1,0:T(8,128)(2,1)} %all-gather.27.cloned.1.call-done), kind=kOutput, calls=%fused_computation.22 | convolution fusion | flops 8602517504 | bytes 25169920 | tf_op jit(solution)/shard_map/dot_general | solution.py:14
  371.8 66.5 %all-gather.29.cloned.1.call-done = bf16[1024,2048]{1,0:T(8,128)(2,1)} async-done(((bf16[256,2048]{1,0:T(8,128)(2,1)}), bf16[1024,2048]{1,0:T(8,128)(2,1)}) %all-gather.29.cloned.1.call-update) | async-done | bytes 4194320 | tf_op jit(solution)/shard_map/all_gather | solution.py:192
  438.3 54.8 %all-gather.33.cloned.1.call-done = bf16[1,2048,2048]{2,1,0:T(8,128)(2,1)} async-done(((bf16[1,256,2048]{2,1,0:T(8,128)(2,1)}), bf16[1,2048,2048]{2,1,0:T(8,128)(2,1)}) %all-gather.33.cloned.1.call-update) | async-done | bytes 8388624 | tf_op jit(solution)/shard_map/all_gather | solution.py:42
  493.1 17.0 %convert_reduce_fusion = (f32[1024]{0:T(1024)}, bf16[2048,1024]{1,0:T(8,128)(2,1)S(1)}) fusion(f32[2048,1024]{1,0:T(8,128)} %get-tuple-element.96, f32[1024]{0:T(1024)S(1)} %bitcast.233, bf16[1024,2048]{1,0:T(8,128)(2,1)} %all-gather.29.cloned.1.call-done, bf16[1,2048,2048]{2,1,0:T(8,128)(2,1)} %all-gather.33.cloned.1.call-done), kind=kOutput, calls=%fused_computation.21 | convolution fusion | flops 8617196544 | bytes 25174016 | tf_op jit(solution)/shard_map/dot_general | solution.py:14
  512.1 10.9 convolution_convert_fusion.2
  523.1 14.6 %convolution_convert_fusion.3 = bf16[2048,2048]{1,0:T(8,128)(2,1)} fusion(bf16[2048,1024]{1,0:T(8,128)(2,1)} %get-tuple-element.95, bf16[1024,2048]{1,0:T(8,128)(2,1)} %all-gather.29.cloned.1.call-done), kind=kOutput, calls=%fused_computation.28 | convolution fusion | flops 8594128896 | bytes 16777216 | tf_op jit(solution)/shard_map/dot_general | solution.py:14
  537.7 14.5 %fusion.21 = bf16[1024,2048]{1,0:T(8,128)(2,1)} fusion(bf16[2048,1024]{1,0:T(8,128)(2,1)} %get-tuple-element.95, bf16[1,2048,2048]{2,1,0:T(8,128)(2,1)} %all-gather.33.cloned.1.call-done), kind=kOutput, calls=%fused_computation.33 | convolution fusion | flops 8592031744 | bytes 16777216 | tf_op jit(solution)/shard_map/dot_general | solution.py:14
  552.3 42.2 %reduce-scatter.11.cloned.1.call-done = bf16[256,2048]{1,0:T(8,128)(2,1)} async-done(((bf16[2048,2048]{1,0:T(8,128)(2,1)}), bf16[256,2048]{1,0:T(8,128)(2,1)}) %reduce-scatter.11.cloned.1.call-update) | async-done | bytes 1048592 | tf_op jit(solution)/shard_map/reduce_scatter | solution.py:46
  597.3 72.2 %reduce-scatter.9.cloned.1.call-done = bf16[256,2048]{1,0:T(8,128)(2,1)} async-done(((bf16[2048,2048]{1,0:T(8,128)(2,1)}), bf16[256,2048]{1,0:T(8,128)(2,1)}) %reduce-scatter.9.cloned.1.call-update) | async-done | bytes 1048592 | tf_op jit(solution)/shard_map/reduce_scatter | solution.py:46
  669.5 4.5 convert_reduce_fusion.6
  675.3 6.5 convolution_convert_fusion.6
  686.8 14.2 %convolution_convert_fusion.4 = bf16[2048,1024]{1,0:T(8,128)(2,1)} fusion(bf16[2048,2048]{1,0:T(8,128)(2,1)} %all-gather.25.cloned.1.call-done, bf16[2048,1024]{1,0:T(8,128)(2,1)} %copy-done.44), kind=kOutput, calls=%fused_computation.34 | convolution fusion | flops 8592031744 | bytes 16777216 | tf_op jit(solution)/shard_map/dot_general | solution.py:14
  704.2 18.3 %fusion.63 = bf16[2,1024,4,64]{1,3,2,0:T(8,128)(2,1)S(1)} fusion(bf16[2,1024,4,64]{1,0,3,2:T(2,128)(2,1)S(1)} %reshape_reshape_transpose_reshape_reshape.3, f32[2,4,1024,1024]{2,3,1,0:T(8,128)} %get-tuple-element.92, f32[2,4,1024]{2,1,0:T(4,128)S(1)} %bitcast.221, f32[4,1024,1024]{1,2,0:T(8,128)} %broadcast_multiply_fusion, ...), kind=kOutput, calls=%fused_computation.89 | convolution fusion | flops 1116209152 | bytes 54558720 | tf_op jit(solution)/shard_map/shqk,sqhe->skhe/dot_general | solution.py:86
  724.8 13.3 %fusion.74 = f32[2,4,1024,1024]{2,3,1,0:T(8,128)} fusion(bf16[2,1024,4,64]{1,3,2,0:T(8,128)(2,1)S(1)} %copy-done.14, bf16[2,1024,4,64]{1,0,3,2:T(2,128)(2,1)S(1)} %reshape_reshape_transpose_reshape_reshape.3), kind=kOutput, calls=%fused_computation.94 | convolution fusion | flops 1073741824 | bytes 35651584 | tf_op jit(solution)/shard_map/sqhe,skhe->shqk/dot_general | solution.py:80
  738.1 55.8 %fusion.66 = bf16[2,1024,4,64]{1,3,2,0:T(8,128)(2,1)} fusion(bf16[2,1024,4,64]{1,3,2,0:T(8,128)(2,1)} %copy.112, f32[2,4,1024,1024]{2,3,1,0:T(8,128)} %fusion.74, f32[2,4,1024,1024]{2,3,1,0:T(8,128)} %get-tuple-element.92, f32[2,4,1024]{2,1,0:T(4,128)S(1)} %bitcast.222, f32[4,1024,1024]{1,2,0:T(8,128)} %broadcast_multiply_fusion, ...), kind=kOutput, calls=%fused_computation.90 | convolution fusion | flops 1183327232 | bytes 88113152 | tf_op jit(solution)/shard_map/shqk,sqhe->skhe/dot_general | solution.py:85
  797.6 54.7 %fusion.69 = bf16[2,1024,4,64]{1,3,2,0:T(8,128)(2,1)} fusion(bf16[2,1024,4,64]{1,3,2,0:T(8,128)(2,1)S(1)} %copy-done.16, f32[2,4,1024,1024]{2,3,1,0:T(8,128)} %fusion.74, f32[2,4,1024,1024]{2,3,1,0:T(8,128)} %get-tuple-element.92, f32[2,4,1024]{2,1,0:T(4,128)S(1)} %bitcast.223, f32[4,1024,1024]{1,2,0:T(8,128)} %broadcast_multiply_fusion, ...), kind=kOutput, calls=%fused_computation.91 | convolution fusion | flops 1183327232 | bytes 88113152 | tf_op jit(solution)/shard_map/shqk,skhe->sqhe/dot_general | solution.py:84
  857.0 10.4 convolution_convert_fusion.5
  867.5 11.8 convolution_convert_fusion.1
  881.2 5.6 convolution_convert_fusion
  887.5 18.8 %all_to_all.32 = bf16[4,128,1024]{2,1,0:T(8,128)(2,1)} all-to-all(bf16[4,128,1024]{2,1,0:T(8,128)(2,1)} %bitcast.220), channel_id=1, replica_groups=mesh['rep'=2,'fsdp'=4,'ctx'=4] {'ctx'}, dimensions={0} | all-to-all | bytes 2097152 | tf_op jit(solution)/shard_map/all_to_all | solution.py:140
  906.3 22.6 %reduce-scatter.15.cloned.1.call-done = bf16[512,768]{1,0:T(8,128)(2,1)} async-done(((bf16[2048,768]{1,0:T(8,128)(2,1)}), bf16[512,768]{1,0:T(8,128)(2,1)}) %reduce-scatter.15.cloned.1.call-update) | async-done | bytes 786448 | tf_op jit(solution)/shard_map/reduce_scatter | solution.py:139
  935.7 8.5 all-to-all-done.4
  945.1 58.4 %reduce-scatter.13.cloned.1.call-done = bf16[256,2048]{1,0:T(8,128)(2,1)} async-done(((bf16[2048,2048]{1,0:T(8,128)(2,1)}), bf16[256,2048]{1,0:T(8,128)(2,1)}) %reduce-scatter.13.cloned.1.call-update) | async-done | bytes 1048592 | tf_op jit(solution)/shard_map/reduce_scatter | solution.py:46
  1006.7 71.9 %reduce-scatter.17.cloned.1.call-done = bf16[256,2048]{1,0:T(8,128)(2,1)} async-done(((bf16[2048,2048]{1,0:T(8,128)(2,1)}), bf16[256,2048]{1,0:T(8,128)(2,1)}) %reduce-scatter.17.cloned.1.call-update) | async-done | bytes 1048592 | tf_op jit(solution)/shard_map/reduce_scatter | solution.py:46
  1079.2 33.9 %all-gather.31.cloned.1.call-done = bf16[512,2048]{1,0:T(8,128)(2,1)} async-done(((bf16[256,2048]{1,0:T(8,128)(2,1)}), bf16[512,2048]{1,0:T(8,128)(2,1)}) %all-gather.31.cloned.1.call-update) | async-done | bytes 2097168 | tf_op jit(solution)/shard_map/all_gather | solution.py:153
  1117.3 30.4 %all-gather.37.cloned.1.call-done = bf16[8,128,1024]{2,1,0:T(8,128)(2,1)} async-done(((bf16[4,128,1024]{2,1,0:T(8,128)(2,1)}), bf16[8,128,1024]{2,1,0:T(8,128)(2,1)}) %all-gather.37.cloned.1.call-update) | async-done | bytes 2097168 | tf_op jit(solution)/shard_map/all_gather | solution.py:141
  1147.7 5.1 reshape.321
  1152.8 7.4 copy.138
  1160.2 6.4 reshape.319
  1166.6 10.3 all-gather.35.cloned.1.call-done
  1188.8 78.7 %all-reduce.4.cloned.1.call-done = f32[16,1536]{1,0:T(8,128)} async-done(((f32[16,1536]{1,0:T(8,128)}), f32[16,1536]{1,0:T(8,128)}) %all-reduce.4.cloned.1.call-update) | async-done | bytes 98320
  1269.0 5.0 psum.7
  1275.1 20.9 %reduce-scatter.19.cloned.1.call-done = bf16[64,2048]{1,0:T(8,128)(2,1)} async-done(((bf16[256,2048]{1,0:T(8,128)(2,1)}), bf16[64,2048]{1,0:T(8,128)(2,1)}) %reduce-scatter.19.cloned.1.call-update) | async-done | bytes 262160 | tf_op jit(solution)/shard_map/reduce_scatter | solution.py:257
  1296.0 8.7 all_gather.64
  (253 shorter events, 135.6 us)
Async XLA Ops:
  7.2 286.6 %copy-start = (bf16[512,2048]{1,0:T(8,128)(2,1)S(1)}, bf16[512,2048]{1,0:T(8,128)(2,1)}, u32[]{:S(2)}) copy-start(bf16[512,2048]{1,0:T(8,128)(2,1)} %param.25) | copy-start | bytes 6291460
  7.2 50.6 %all-gather.21.cloned.1.call-start = ((), (), s32[]{:S(2)}) async-start(), calls=%async_computation.16 | async-start | bytes 1310720 | tf_op jit(solution)/shard_map/all_gather | solution.py:189
  9.1 97.1 %all-gather.19.cloned.1.call-start = ((), (), s32[]{:S(2)}) async-start(), calls=%async_computation.15 | async-start | bytes 3932160 | tf_op jit(solution)/shard_map/all_gather | solution.py:136
  11.7 19.9 %copy-start.34 = (bf16[128]{0:T(256)(128)(2,1)S(1)}, bf16[128]{0:T(256)(128)(2,1)}, u32[]{:S(2)}) copy-start(bf16[128]{0:T(256)(128)(2,1)} %param.28) | copy-start | bytes 772
  11.7 20.1 %copy-start.35 = (bf16[128]{0:T(256)(128)(2,1)S(1)}, bf16[128]{0:T(256)(128)(2,1)}, u32[]{:S(2)}) copy-start(bf16[128]{0:T(256)(128)(2,1)} %param.29) | copy-start | bytes 772
  11.7 20.3 %copy-start.36 = (bf16[128]{0:T(256)(128)(2,1)S(1)}, bf16[128]{0:T(256)(128)(2,1)}, u32[]{:S(2)}) copy-start(bf16[128]{0:T(256)(128)(2,1)} %param.30) | copy-start | bytes 772
  11.7 20.5 %copy-start.37 = (bf16[128]{0:T(256)(128)(2,1)S(1)}, bf16[128]{0:T(256)(128)(2,1)}, u32[]{:S(2)}) copy-start(bf16[128]{0:T(256)(128)(2,1)} %param.22) | copy-start | bytes 772
  11.7 20.7 %copy-start.38 = (bf16[128]{0:T(256)(128)(2,1)S(1)}, bf16[128]{0:T(256)(128)(2,1)}, u32[]{:S(2)}) copy-start(bf16[128]{0:T(256)(128)(2,1)} %param.26) | copy-start | bytes 772
  11.8 21.0 %copy-start.39 = (bf16[128]{0:T(256)(128)(2,1)S(1)}, bf16[128]{0:T(256)(128)(2,1)}, u32[]{:S(2)}) copy-start(bf16[128]{0:T(256)(128)(2,1)} %param.19) | copy-start | bytes 772
  11.8 21.2 %copy-start.40 = (bf16[128]{0:T(256)(128)(2,1)S(1)}, bf16[128]{0:T(256)(128)(2,1)}, u32[]{:S(2)}) copy-start(bf16[128]{0:T(256)(128)(2,1)} %param.20) | copy-start | bytes 772
  11.8 21.4 %copy-start.32 = (bf16[512]{0:T(512)(128)(2,1)S(1)}, bf16[512]{0:T(512)(128)(2,1)}, u32[]{:S(2)}) copy-start(bf16[512]{0:T(512)(128)(2,1)} %param.24) | copy-start | bytes 3076
  11.8 42.6 %copy-start.6 = (bf16[1,256,2048]{2,1,0:T(8,128)(2,1)S(1)}, bf16[1,256,2048]{2,1,0:T(8,128)(2,1)}, u32[]{:S(2)}) copy-start(bf16[1,256,2048]{2,1,0:T(8,128)(2,1)} %param.16) | copy-start | bytes 3145732
  31.3 130.4 %all-gather.17.cloned.1.call-start = ((), (), s32[]{:S(2)}) async-start(), calls=%async_computation.14 | async-start | bytes 9437184 | tf_op jit(solution)/shard_map/all_gather | solution.py:42
  57.7 227.1 %all-gather.23.cloned.1.call-start = ((), (), s32[]{:S(2)}) async-start(), calls=%async_computation.17 | async-start | bytes 9437184 | tf_op jit(solution)/shard_map/all_gather | solution.py:42
  69.2 24.2 %all-to-all-start.2 = ((bf16[4,128,1024]{1,2,0:T(8,128)(2,1)}), bf16[4,128,1024]{1,2,0:T(8,128)(2,1)}, u32[]{:S(2)}, u32[]{:S(2)}) async-start(bf16[4,128,1024]{1,2,0:T(8,128)(2,1)} %bitcast.209), calls=%async_computation.2 | async-start | bytes 2097152 | tf_op jit(solution)/shard_map/all_to_all | solution.py:135
  73.5 227.1 %all-gather.27.cloned.1.call-start = ((), (), s32[]{:S(2)}) async-start(), calls=%async_computation.19 | async-start | bytes 5242880 | tf_op jit(solution)/shard_map/all_gather | solution.py:136
  95.8 260.2 %all-gather.25.cloned.1.call-start = ((), (), s32[]{:S(2)}) async-start(), calls=%async_computation.18 | async-start | bytes 9437184 | tf_op jit(solution)/shard_map/all_gather | solution.py:42
  200.1 22.8 %copy-start.2 = (pred[2,1024,1024]{1,2,0:T(8,128)(4,1)S(1)}, pred[2,1024,1024]{1,2,0:T(8,128)(4,1)}, u32[]{:S(2)}) copy-start(pred[2,1024,1024]{1,2,0:T(8,128)(4,1)} %broadcast_or_fusion) | copy-start | bytes 6291460
  293.7 144.6 %all-gather.29.cloned.1.call-start = ((), (), s32[]{:S(2)}) async-start(), calls=%async_computation.20 | async-start | bytes 5242880 | tf_op jit(solution)/shard_map/all_gather | solution.py:192
  295.0 198.2 %all-gather.33.cloned.1.call-start = ((), (), s32[]{:S(2)}) async-start(), calls=%async_computation.30 | async-start | bytes 9437184 | tf_op jit(solution)/shard_map/all_gather | solution.py:42
  295.7 298.8 %reduce-scatter.11.cloned.1.call-start = ((), (), s32[]{:S(2)}) async-start(), calls=%async_computation.22 | async-start | bytes 9437184 | tf_op jit(solution)/shard_map/reduce_scatter | solution.py:46
  523.1 146.4 %reduce-scatter.9.cloned.1.call-start = ((), (), s32[]{:S(2)}) async-start(), calls=%async_computation.21 | async-start | bytes 9437184 | tf_op jit(solution)/shard_map/reduce_scatter | solution.py:46
  537.7 349.2 %reduce-scatter.23.cloned.1.call-start = ((), (), s32[]{:S(2)}) async-start(), calls=%async_computation.28 | async-start | bytes 5242880 | tf_op jit(solution)/shard_map/reduce_scatter | solution.py:253
  552.2 42.2 %copy-start.5 = (f32[256,2048]{1,0:T(8,128)S(1)}, f32[256,2048]{1,0:T(8,128)}, u32[]{:S(2)}) copy-start(f32[256,2048]{1,0:T(8,128)} %copy-done.4) | copy-start | bytes 6291460
  552.2 117.2 %copy-start.11 = (bf16[1,256,2048]{2,1,0:T(8,128)(2,1)S(1)}, bf16[1,256,2048]{2,1,0:T(8,128)(2,1)}, u32[]{:S(2)}) copy-start(bf16[1,256,2048]{2,1,0:T(8,128)(2,1)} %param.31) | copy-start | bytes 3145732
  552.2 117.2 %copy-start.23 = (f32[2048]{0:T(1024)S(1)}, f32[2048]{0:T(1024)}, u32[]{:S(2)}) copy-start(f32[2048]{0:T(1024)} %get-tuple-element.73) | copy-start | bytes 24580
  683.2 17.9 %all-to-all-start.3 = ((bf16[8,256,256]{1,2,0:T(8,128)(2,1)}), bf16[8,256,256]{1,2,0:T(8,128)(2,1)S(1)}, u32[]{:S(2)}, u32[]{:S(2)}) async-start(bf16[8,256,256]{1,2,0:T(8,128)(2,1)} %bitcast.29), calls=%async_computation.5 | async-start | bytes 2097152 | tf_op jit(solution)/shard_map/all_to_all | solution.py:50
  686.7 200.7 %reduce-scatter.21.cloned.1.call-start = ((), (), s32[]{:S(2)}) async-start(), calls=%async_computation.27 | async-start | bytes 5242880 | tf_op jit(solution)/shard_map/reduce_scatter | solution.py:139
  701.0 227.9 %reduce-scatter.15.cloned.1.call-start = ((), (), s32[]{:S(2)}) async-start(), calls=%async_computation.24 | async-start | bytes 3932160 | tf_op jit(solution)/shard_map/reduce_scatter | solution.py:139
  867.4 136.2 %reduce-scatter.13.cloned.1.call-start = ((), (), s32[]{:S(2)}) async-start(), calls=%async_computation.23 | async-start | bytes 9437184 | tf_op jit(solution)/shard_map/reduce_scatter | solution.py:46
  879.3 199.3 %reduce-scatter.17.cloned.1.call-start = ((), (), s32[]{:S(2)}) async-start(), calls=%async_computation.25 | async-start | bytes 9437184 | tf_op jit(solution)/shard_map/reduce_scatter | solution.py:46
  886.8 45.8 %copy-start.12 = (bf16[1,256,2048]{2,1,0:T(8,128)(2,1)S(1)}, bf16[1,256,2048]{2,1,0:T(8,128)(2,1)}, u32[]{:S(2)}) copy-start(bf16[1,256,2048]{2,1,0:T(8,128)(2,1)} %param.31) | copy-start | bytes 3145732
  886.8 46.0 %copy-start.31 = (f32[1024]{0:T(1024)S(1)}, f32[1024]{0:T(1024)}, u32[]{:S(2)}) copy-start(f32[1024]{0:T(1024)} %get-tuple-element.97) | copy-start | bytes 12292
  886.8 226.3 %all-gather.31.cloned.1.call-start = ((), (), s32[]{:S(2)}) async-start(), calls=%async_computation.29 | async-start | bytes 3145728 | tf_op jit(solution)/shard_map/all_gather | solution.py:153
  887.4 260.3 %all-gather.37.cloned.1.call-start = ((), (), s32[]{:S(2)}) async-start(), calls=%async_computation.32 | async-start | bytes 3145728 | tf_op jit(solution)/shard_map/all_gather | solution.py:141
  906.3 97.3 %copy-start.7 = (bf16[1,256,2048]{2,1,0:T(8,128)(2,1)S(1)}, bf16[1,256,2048]{2,1,0:T(8,128)(2,1)}, u32[]{:S(2)}) copy-start(bf16[1,256,2048]{2,1,0:T(8,128)(2,1)} %param.16) | copy-start | bytes 3145732
  906.3 97.3 %copy-start.21 = (f32[2048]{0:T(1024)S(1)}, f32[2048]{0:T(1024)}, u32[]{:S(2)}) copy-start(f32[2048]{0:T(1024)} %copy-done.20) | copy-start | bytes 24580
  906.3 97.3 %copy-start.28 = (f32[256]{0:T(256)S(1)}, f32[256]{0:T(256)}, u32[]{:S(2)}) copy-start(f32[256]{0:T(256)} %copy-done.27) | copy-start | bytes 3076
  906.3 97.3 %copy-start.30 = (f32[256]{0:T(256)S(1)}, f32[256]{0:T(256)}, u32[]{:S(2)}) copy-start(f32[256]{0:T(256)} %copy-done.29) | copy-start | bytes 3076
  928.9 77.0 %copy-start.25 = (f32[2048]{0:T(1024)S(1)}, f32[2048]{0:T(1024)}, u32[]{:S(2)}) copy-start(f32[2048]{0:T(1024)} %get-tuple-element.60) | copy-start | bytes 24580
  928.9 77.0 %copy-start.24 = (f32[2048]{0:T(1024)S(1)}, f32[2048]{0:T(1024)}, u32[]{:S(2)}) copy-start(f32[2048]{0:T(1024)} %get-tuple-element.66) | copy-start | bytes 24580
  928.9 77.0 %copy-start.26 = (f32[2048]{0:T(1024)S(1)}, f32[2048]{0:T(1024)}, u32[]{:S(2)}) copy-start(f32[2048]{0:T(1024)} %get-tuple-element.68) | copy-start | bytes 24580
  928.9 15.3 %all-to-all-start.4 = ((bf16[4,128,768]{2,1,0:T(8,128)(2,1)}), bf16[4,128,768]{2,1,0:T(8,128)(2,1)S(1)}, u32[]{:S(2)}, u32[]{:S(2)}) async-start(bf16[4,128,768]{2,1,0:T(8,128)(2,1)} %bitcast.224), calls=%async_computation.8 | async-start | bytes 1572864 | tf_op jit(solution)/shard_map/all_to_all | solution.py:140
  932.6 146.1 %copy-start.42 = (u32[32]{0:T(128)S(1)}, u32[32]{0:T(128)}, u32[]{:S(2)}) copy-start(u32[32]{0:T(128)} %constant.196) | copy-start | bytes 388
  932.6 244.3 %all-gather.35.cloned.1.call-start = ((), (), s32[]{:S(2)}) async-start(), calls=%async_computation.31 | async-start | bytes 2359296 | tf_op jit(solution)/shard_map/all_gather | solution.py:141
  945.1 322.4 %all-reduce.4.cloned.1.call-start = ((), (), s32[]{:S(2)}) async-start(), calls=%async_computation.33 | async-start | bytes 196608
  1006.7 289.3 %reduce-scatter.19.cloned.1.call-start = ((), (), s32[]{:S(2)}) async-start(), calls=%async_computation.26 | async-start | bytes 1310720 | tf_op jit(solution)/shard_map/reduce_scatter | solution.py:257
  1184.6 121.2 %copy-start.1 = (bf16[512,2048]{1,0:T(8,128)(2,1)S(1)}, bf16[512,2048]{1,0:T(8,128)(2,1)}, u32[]{:S(2)}) copy-start(bf16[512,2048]{1,0:T(8,128)(2,1)} %param.25) | copy-start | bytes 6291460
  (20 other events, 111.4 us)
Sparse Core Ops, SparseCore 0:
  10.2 30.7 all-gather.20
  43.1 63.0 all-gather.18
  108.6 53.0 all-gather.16
  163.5 54.3 all-gather.22
  219.9 80.7 all-gather.26
  303.0 52.9 all-gather.24
  357.5 80.7 all-gather.28
  440.2 52.9 all-gather.32
  523.2 71.2 reduce-scatter.10
  598.2 71.2 reduce-scatter.8
  671.8 76.7 reduce-scatter.22
  751.4 77.2 reduce-scatter.20
  867.5 61.3 reduce-scatter.14
  932.2 71.2 reduce-scatter.12
  1007.3 71.2 reduce-scatter.16
  1080.0 33.0 all-gather.30
  1114.5 33.1 all-gather.36
  1149.7 27.1 all-gather.34
  1180.3 87.1 all-reduce.3
  1269.8 26.1 reduce-scatter.18
where the time goes:
time: 1320 us; the launch traced here: 1310 us
  waiting for transfers between devices  699 us (53%)
  matrix products  322 us (24%)
  local copies, waits for them, and re-layouts  112 us (8%)
  blocking collectives  91.5 us (7%)
  other arithmetic  59.9 us (5%)
  between operations  15.9 us (1%)
    reduce_scatter x4, waiting for transfers between devices, scatter_tp(): return lax.psum_scatter(x, TP, scatter_dimension=0, tiled=True)  245 us
    all_gather x4, waiting for transfers between devices, gather_tp(): return lax.all_gather(x, TP, axis=0, tiled=True)  166 us
    dot_general x12, matrix products, dot(): lax.dot_general(a, b, (((ca,), (cb,)), ((), ())), preferred_element_type=...  138 us
    unnamed x21, waiting for transfers between devices  80.7 us
    all_gather x1, waiting for transfers between devices, shards(): lax.all_gather(half_rows(shrink_weight), 'fsdp', axis=0, tiled=True)  66.5 us
    dot_general x1, matrix products, attention_backward(): jnp.einsum('shqk,sqhe->skhe', d_raw, q, preferred_element_type=F32)  55.8 us
    dot_general x1, matrix products, attention_backward(): jnp.einsum('shqk,skhe->sqhe', d_raw, k, preferred_element_type=F32)  54.7 us
    all_gather x2, waiting for transfers between devices, join_columns(): both = lax.all_gather(blocks, 'rep', axis=0, tiled=False)  40.7 us
  transfers between devices with their start and end apart: 23, of which 18 were waited for; matrix products, arithmetic and copies ran while one was open for 35% of the time, Pallas kernels for 0%

commit v1 on v0

--- a/solution.py
+++ b/solution.py
@@ -189,7 +189,16 @@
         lax.all_gather(half_rows(dense_weight), "fsdp", axis=0, tiled=True) if aligned else None
     )
     expand_cols = columns(expand_weight, 1)
-    shrink_rows = lax.all_gather(half_rows(shrink_weight), "fsdp", axis=0, tiled=True)
+    shard = half_rows(shrink_weight)
+    ways, here, step_2 = (lax.axis_size("fsdp"), lax.axis_index("fsdp"), shard.shape[0])
+    line, have = (shard, 1)
+    while have < ways:
+        line = jnp.concatenate(
+            [line, lax.ppermute(line, "fsdp", [(d, (d - have) % ways) for d in range(ways)])],
+            axis=0,
+        )
+        have = 2 * have
+    shrink_rows = jnp.roll(line, here * step_2, axis=0)
     if aligned:
         dense_all = gather_tp(dense_rows)
     else:

time: 1320 us -> 1280 us (0.970)
  waiting for transfers between devices: 699 us -> 638 us
    ppermute x0 -> x2, waiting for transfers between devices: none -> 112 us  [shards(): lax.ppermute(line, 'fsdp', [(d, (d - have) % ways) for d in range(ways)])]
    all_gather x4, waiting for transfers between devices: 166 us -> 55.5 us  [gather_tp(): return lax.all_gather(x, TP, axis=0, tiled=True)]
    all_gather x1 -> x0, waiting for transfers between devices: 66.5 us -> none  [shards(): lax.all_gather(half_rows(shrink_weight), 'fsdp', axis=0, tiled=True)]
    unnamed x122 -> x123, local copies, waits for them, and re-layouts: 28.3 us -> 39.3 us
    unnamed x21 -> x20, waiting for transfers between devices: 80.7 us -> 80.9 us
  transfers between devices with their start and end apart: 23 -> 24, of which waited for: 18 -> 16; matrix products, arithmetic and copies ran while one was open for 35% -> 37% of each run, Pallas kernels for 0% -> 0%
where the time goes in v1:
time: 1280 us; the launch traced here: 1270 us
  waiting for transfers between devices  638 us (50%)
  matrix products  323 us (25%)
  local copies, waits for them, and re-layouts  121 us (9%)
  blocking collectives  91.2 us (7%)
  other arithmetic  61.7 us (5%)
  starting transfers between devices  18.5 us (1%)
  between operations  15.6 us (1%)
    reduce_scatter x4, waiting for transfers between devices, scatter_tp(): return lax.psum_scatter(x, TP, scatter_dimension=0, tiled=True)  244 us
    dot_general x12, matrix products, dot(): lax.dot_general(a, b, (((ca,), (cb,)), ((), ())), preferred_element_type=...  140 us
    ppermute x2, waiting for transfers between devices, shards(): lax.ppermute(line, 'fsdp', [(d, (d - have) % ways) for d in range(ways)])  112 us
    unnamed x20, waiting for transfers between devices  80.9 us
    dot_general x1, matrix products, attention_backward(): jnp.einsum('shqk,sqhe->skhe', d_raw, q, preferred_element_type=F32)  55.8 us
    all_gather x4, waiting for transfers between devices, gather_tp(): return lax.all_gather(x, TP, axis=0, tiled=True)  55.5 us
    dot_general x1, matrix products, attention_backward(): jnp.einsum('shqk,skhe->sqhe', d_raw, k, preferred_element_type=F32)  55 us
    all_gather x2, waiting for transfers between devices, join_columns(): both = lax.all_gather(blocks, 'rep', axis=0, tiled=False)  40.7 us
  transfers between devices with their start and end apart: 24, of which 16 were waited for; matrix products, arithmetic and copies ran while one was open for 37% of the time, Pallas kernels for 0%

profile of v1, /device:TPU:0, one launch (start us, length us, event | category | flops | bytes accessed | tf_op | source)
XLA Modules:
  0.0 1269.6 jit_solution(397846810492300005)
XLA Ops:
  11.1 15.7 %all_to_all.30 = bf16[4,128,768]{1,2,0:T(8,128)(2,1)S(1)} all-to-all(bf16[4,128,768]{1,2,0:T(8,128)(2,1)S(1)} %bitcast.217), channel_id=1, replica_groups=mesh['rep'=2,'fsdp'=4,'ctx'=4] {'ctx'}, dimensions={0} | all-to-all | bytes 1572864 | tf_op jit(solution)/shard_map/all_to_all | solution.py:135
  29.8 21.0 %all-gather.4 = bf16[16,1,1536]{2,1,0:T(2,128)(2,1)S(1)} all-gather(bf16[1,1,1536]{2,1,0:T(2,128)(2,1)S(1)} %reshape.335), channel_id=2, replica_groups=mesh['rep'=2,'fsdp'=4,'ctx'=4] {'fsdp','ctx'}, dimensions={0}, use_global_device_ids=true | all-gather | bytes 52224 | tf_op jit(solution)/shard_map/all_gather | solution.py:168
  68.3 8.1 broadcast_multiply_fusion
  87.2 19.2 %all-gather.18.cloned.1.call-done = bf16[2048,768]{1,0:T(8,128)(2,1)} async-done(((bf16[512,768]{1,0:T(8,128)(2,1)}), bf16[2048,768]{1,0:T(8,128)(2,1)}) %all-gather.18.cloned.1.call-update) | async-done | bytes 3145744 | tf_op jit(solution)/shard_map/all_gather | solution.py:136
  106.4 55.5 %all-gather.16.cloned.1.call-done = bf16[2048,2048]{1,0:T(8,128)(2,1)} async-done(((bf16[256,2048]{1,0:T(8,128)(2,1)}), bf16[2048,2048]{1,0:T(8,128)(2,1)}) %all-gather.16.cloned.1.call-update) | async-done | bytes 8388624 | tf_op jit(solution)/shard_map/all_gather | solution.py:42
  162.0 10.0 fusion.97
  174.8 4.4 reshape.343
  183.3 4.4 reshape.344
  191.8 4.5 reshape.342
  200.4 20.2 %select_reduce_fusion = (f32[2,4,1024]{2,1,0:T(4,128)S(1)}, f32[2,4,1024,1024]{2,3,1,0:T(8,128)}) fusion(f32[4,1024,1024]{1,2,0:T(8,128)} %broadcast_multiply_fusion, pred[2,1024,1024]{1,2,0:T(8,128)(4,1)S(1)} %broadcast_or_fusion, bf16[2,1024,4,64]{1,3,2,0:T(8,128)(2,1)} %copy.112, bf16[2,1024,4,64]{1,3,2,0:T(8,128)(2,1)} %copy.113), kind=kOutput, calls=%fused_computation.8 | convolution fusion | flops 1107288064 | bytes 54558720 | tf_op jit(solution)/shard_map/sqhe,skhe->shqk/dot_general | solution.py:54
  220.5 18.9 %fusion.4 = f32[2,4,1024]{2,1,0:T(4,128)S(1)} fusion(f32[2,4,1024,1024]{2,3,1,0:T(8,128)} %get-tuple-element.94, f32[2,4,1024]{2,1,0:T(4,128)S(1)} %get-tuple-element.93, f32[4,1024,1024]{1,2,0:T(8,128)} %broadcast_multiply_fusion, pred[2,1024,1024]{1,2,0:T(8,128)(4,1)S(1)} %broadcast_or_fusion), kind=kLoop, calls=%fused_computation.9 | loop fusion | flops 41934848 | bytes 52494336 | tf_op jit(solution)/shard_map/reduce_sum | solution.py:71
  239.4 19.5 %fusion.74 = bf16[2,1024,4,64]{1,3,2,0:T(8,128)(2,1)S(1)} fusion(bf16[2,1024,4,64]{1,3,2,0:T(8,128)(2,1)S(1)} %copy-done.12, f32[2,4,1024,1024]{2,3,1,0:T(8,128)} %get-tuple-element.94, f32[2,4,1024]{2,1,0:T(4,128)S(1)} %fusion.4, f32[2,4,1024]{2,1,0:T(4,128)S(1)} %get-tuple-element.93, f32[4,1024,1024]{1,2,0:T(8,128)} %broadcast_multiply_fusion, ...), kind=kOutput, calls=%fused_computation.95 | convolution fusion | flops 1124597760 | bytes 54591488 | tf_op jit(solution)/shard_map/shqk,skhe->sqhe/dot_general | solution.py:73
  264.6 17.7 %all_to_all.31 = bf16[8,256,256]{1,2,0:T(8,128)(2,1)} all-to-all(bf16[8,256,256]{1,2,0:T(8,128)(2,1)S(1)} %copy.117), channel_id=1, replica_groups=mesh['rep'=2,'fsdp'=4,'ctx'=4] {'rep','ctx'}, dimensions={0} | all-to-all | bytes 2097152 | tf_op jit(solution)/shard_map/all_to_all | solution.py:50
  282.3 6.4 fusion.96
  298.0 23.9 %collective-permute-done = bf16[256,2048]{1,0:T(8,128)(2,1)S(1)} collective-permute-done((bf16[256,2048]{1,0:T(8,128)(2,1)S(1)}, bf16[256,2048]{1,0:T(8,128)(2,1)S(1)}, u32[]{:S(2)}, u32[]{:S(2)}) %collective-permute-start) | collective-permute-done | bytes 1048608 | tf_op jit(solution)/shard_map/ppermute | solution.py:197
  328.1 88.4 %collective-permute-done.1 = bf16[512,2048]{1,0:T(8,128)(2,1)} collective-permute-done((bf16[512,2048]{1,0:T(8,128)(2,1)}, bf16[512,2048]{1,0:T(8,128)(2,1)}, u32[]{:S(2)}, u32[]{:S(2)}) %collective-permute-start.1) | collective-permute-done | bytes 2097184 | tf_op jit(solution)/shard_map/ppermute | solution.py:197
  426.3 15.9 %multiply_convert_fusion.1 = (bf16[2048,1024]{1,0:T(8,128)(2,1)}, f32[2048,1024]{1,0:T(8,128)}) fusion(f32[1024]{0:T(1024)S(1)} %bitcast.230, bf16[2048,2048]{1,0:T(8,128)(2,1)} %all-gather.24.cloned.1.call-done, bf16[2048,1024]{1,0:T(8,128)(2,1)} %all-gather.26.cloned.1.call-done), kind=kOutput, calls=%fused_computation.22 | convolution fusion | flops 8602517504 | bytes 25169920 | tf_op jit(solution)/shard_map/dot_general | solution.py:14
  442.2 17.0 %convert_reduce_fusion = (f32[1024]{0:T(1024)}, bf16[2048,1024]{1,0:T(8,128)(2,1)S(1)}) fusion(f32[2048,1024]{1,0:T(8,128)} %get-tuple-element.98, f32[1024]{0:T(1024)S(1)} %bitcast.231, bf16[1,2048,2048]{2,1,0:T(8,128)(2,1)} %all-gather.30.cloned.1.call-done, bf16[2048,2048]{1,0:T(8,128)(2,1)} %constant_dynamic-update-slice_fusion, s32[]{:T(128)S(6)} %select_n.66), kind=kOutput, calls=%fused_computation.21 | convolution fusion | flops 8617196544 | bytes 25174020 | tf_op jit(solution)/shard_map/dot_general | solution.py:14
  461.2 10.9 convolution_convert_fusion.2
  472.2 14.6 %convolution_convert_fusion.3 = bf16[2048,2048]{1,0:T(8,128)(2,1)} fusion(bf16[2048,1024]{1,0:T(8,128)(2,1)} %get-tuple-element.97, bf16[2048,2048]{1,0:T(8,128)(2,1)} %constant_dynamic-update-slice_fusion, s32[]{:T(128)S(6)} %select_n.66), kind=kOutput, calls=%fused_computation.28 | convolution fusion | flops 8594128896 | bytes 16777220 | tf_op jit(solution)/shard_map/dot_general | solution.py:14
  486.9 14.4 %fusion.21 = bf16[1024,2048]{1,0:T(8,128)(2,1)} fusion(bf16[2048,1024]{1,0:T(8,128)(2,1)} %get-tuple-element.97, bf16[1,2048,2048]{2,1,0:T(8,128)(2,1)} %all-gather.30.cloned.1.call-done), kind=kOutput, calls=%fused_computation.33 | convolution fusion | flops 8592031744 | bytes 16777216 | tf_op jit(solution)/shard_map/dot_general | solution.py:14
  501.4 42.1 %reduce-scatter.11.cloned.1.call-done = bf16[256,2048]{1,0:T(8,128)(2,1)} async-done(((bf16[2048,2048]{1,0:T(8,128)(2,1)}), bf16[256,2048]{1,0:T(8,128)(2,1)}) %reduce-scatter.11.cloned.1.call-update) | async-done | bytes 1048592 | tf_op jit(solution)/shard_map/reduce_scatter | solution.py:46
  547.0 71.7 %reduce-scatter.9.cloned.1.call-done = bf16[256,2048]{1,0:T(8,128)(2,1)} async-done(((bf16[2048,2048]{1,0:T(8,128)(2,1)}), bf16[256,2048]{1,0:T(8,128)(2,1)}) %reduce-scatter.9.cloned.1.call-update) | async-done | bytes 1048592 | tf_op jit(solution)/shard_map/reduce_scatter | solution.py:46
  618.7 5.5 convert_reduce_fusion.6
  625.5 7.5 convolution_convert_fusion.6
  639.6 14.2 %convolution_convert_fusion.4 = bf16[2048,1024]{1,0:T(8,128)(2,1)} fusion(bf16[2048,2048]{1,0:T(8,128)(2,1)} %all-gather.24.cloned.1.call-done, bf16[2048,1024]{1,0:T(8,128)(2,1)} %copy-done.42), kind=kOutput, calls=%fused_computation.34 | convolution fusion | flops 8592031744 | bytes 16777216 | tf_op jit(solution)/shard_map/dot_general | solution.py:14
  659.1 19.0 %fusion.65 = bf16[2,1024,4,64]{1,3,2,0:T(8,128)(2,1)S(1)} fusion(bf16[2,1024,4,64]{1,0,3,2:T(2,128)(2,1)} %reshape_reshape_transpose_reshape_reshape.3, f32[2,4,1024,1024]{2,3,1,0:T(8,128)} %get-tuple-element.94, f32[2,4,1024]{2,1,0:T(4,128)S(1)} %bitcast.219, f32[4,1024,1024]{1,2,0:T(8,128)} %broadcast_multiply_fusion, ...), kind=kOutput, calls=%fused_computation.92 | convolution fusion | flops 1116209152 | bytes 54558720 | tf_op jit(solution)/shard_map/shqk,sqhe->skhe/dot_general | solution.py:86
  680.4 13.3 %fusion.76 = f32[2,4,1024,1024]{2,3,1,0:T(8,128)} fusion(bf16[2,1024,4,64]{1,3,2,0:T(8,128)(2,1)S(1)} %copy-done.13, bf16[2,1024,4,64]{1,0,3,2:T(2,128)(2,1)S(1)} %copy-done.7), kind=kOutput, calls=%fused_computation.97 | convolution fusion | flops 1073741824 | bytes 35651584 | tf_op jit(solution)/shard_map/sqhe,skhe->shqk/dot_general | solution.py:80
  693.7 55.8 %fusion.68 = bf16[2,1024,4,64]{1,3,2,0:T(8,128)(2,1)} fusion(bf16[2,1024,4,64]{1,3,2,0:T(8,128)(2,1)} %copy.112, f32[2,4,1024,1024]{2,3,1,0:T(8,128)} %fusion.76, f32[2,4,1024,1024]{2,3,1,0:T(8,128)} %get-tuple-element.94, f32[2,4,1024]{2,1,0:T(4,128)S(1)} %bitcast.220, f32[4,1024,1024]{1,2,0:T(8,128)} %broadcast_multiply_fusion, ...), kind=kOutput, calls=%fused_computation.93 | convolution fusion | flops 1183327232 | bytes 88113152 | tf_op jit(solution)/shard_map/shqk,sqhe->skhe/dot_general | solution.py:85
  753.1 55.0 %fusion.71 = bf16[2,1024,4,64]{1,3,2,0:T(8,128)(2,1)} fusion(bf16[2,1024,4,64]{1,3,2,0:T(8,128)(2,1)} %copy.113, f32[2,4,1024,1024]{2,3,1,0:T(8,128)} %fusion.76, f32[2,4,1024,1024]{2,3,1,0:T(8,128)} %get-tuple-element.94, f32[2,4,1024]{2,1,0:T(4,128)S(1)} %bitcast.221, f32[4,1024,1024]{1,2,0:T(8,128)} %broadcast_multiply_fusion, ...), kind=kOutput, calls=%fused_computation.94 | convolution fusion | flops 1183327232 | bytes 88113152 | tf_op jit(solution)/shard_map/shqk,skhe->sqhe/dot_general | solution.py:84
  813.9 10.4 convolution_convert_fusion.5
  824.4 11.8 convolution_convert_fusion.1
  837.8 6.8 convolution_convert_fusion
  845.4 18.8 %all_to_all.32 = bf16[4,128,1024]{2,1,0:T(8,128)(2,1)} all-to-all(bf16[4,128,1024]{2,1,0:T(8,128)(2,1)} %bitcast.218), channel_id=1, replica_groups=mesh['rep'=2,'fsdp'=4,'ctx'=4] {'ctx'}, dimensions={0} | all-to-all | bytes 2097152 | tf_op jit(solution)/shard_map/all_to_all | solution.py:140
  864.2 21.7 %reduce-scatter.15.cloned.1.call-done = bf16[512,768]{1,0:T(8,128)(2,1)} async-done(((bf16[2048,768]{1,0:T(8,128)(2,1)}), bf16[512,768]{1,0:T(8,128)(2,1)}) %reduce-scatter.15.cloned.1.call-update) | async-done | bytes 786448 | tf_op jit(solution)/shard_map/reduce_scatter | solution.py:139
  892.5 8.5 all-to-all-done.4
  902.0 58.7 %reduce-scatter.13.cloned.1.call-done = bf16[256,2048]{1,0:T(8,128)(2,1)} async-done(((bf16[2048,2048]{1,0:T(8,128)(2,1)}), bf16[256,2048]{1,0:T(8,128)(2,1)}) %reduce-scatter.13.cloned.1.call-update) | async-done | bytes 1048592 | tf_op jit(solution)/shard_map/reduce_scatter | solution.py:46
  963.8 71.9 %reduce-scatter.17.cloned.1.call-done = bf16[256,2048]{1,0:T(8,128)(2,1)} async-done(((bf16[2048,2048]{1,0:T(8,128)(2,1)}), bf16[256,2048]{1,0:T(8,128)(2,1)}) %reduce-scatter.17.cloned.1.call-update) | async-done | bytes 1048592 | tf_op jit(solution)/shard_map/reduce_scatter | solution.py:46
  1036.3 33.9 %all-gather.28.cloned.1.call-done = bf16[512,2048]{1,0:T(8,128)(2,1)} async-done(((bf16[256,2048]{1,0:T(8,128)(2,1)}), bf16[512,2048]{1,0:T(8,128)(2,1)}) %all-gather.28.cloned.1.call-update) | async-done | bytes 2097168 | tf_op jit(solution)/shard_map/all_gather | solution.py:153
  1074.4 30.4 %all-gather.34.cloned.1.call-done = bf16[8,128,1024]{2,1,0:T(8,128)(2,1)} async-done(((bf16[4,128,1024]{2,1,0:T(8,128)(2,1)}), bf16[8,128,1024]{2,1,0:T(8,128)(2,1)}) %all-gather.34.cloned.1.call-update) | async-done | bytes 2097168 | tf_op jit(solution)/shard_map/all_gather | solution.py:141
  1104.8 5.1 reshape.321
  1109.9 7.4 copy.138
  1117.3 6.4 reshape.319
  1123.7 10.3 all-gather.32.cloned.1.call-done
  1145.5 79.0 %all-reduce.4.cloned.1.call-done = f32[16,1536]{1,0:T(8,128)} async-done(((f32[16,1536]{1,0:T(8,128)}), f32[16,1536]{1,0:T(8,128)}) %all-reduce.4.cloned.1.call-update) | async-done | bytes 98320
  1225.9 5.0 psum.7
  1232.0 21.0 %reduce-scatter.19.cloned.1.call-done = bf16[64,2048]{1,0:T(8,128)(2,1)} async-done(((bf16[256,2048]{1,0:T(8,128)(2,1)}), bf16[64,2048]{1,0:T(8,128)(2,1)}) %reduce-scatter.19.cloned.1.call-update) | async-done | bytes 262160 | tf_op jit(solution)/shard_map/reduce_scatter | solution.py:266
  1253.1 8.7 all_gather.60
  (256 shorter events, 143.2 us)
Async XLA Ops:
  7.2 21.3 %copy-start.33 = (bf16[128]{0:T(256)(128)(2,1)S(1)}, bf16[128]{0:T(256)(128)(2,1)}, u32[]{:S(2)}) copy-start(bf16[128]{0:T(256)(128)(2,1)} %param.29) | copy-start | bytes 772
  7.2 21.5 %copy-start.34 = (bf16[128]{0:T(256)(128)(2,1)S(1)}, bf16[128]{0:T(256)(128)(2,1)}, u32[]{:S(2)}) copy-start(bf16[128]{0:T(256)(128)(2,1)} %param.30) | copy-start | bytes 772
  7.2 21.7 %copy-start.35 = (bf16[128]{0:T(256)(128)(2,1)S(1)}, bf16[128]{0:T(256)(128)(2,1)}, u32[]{:S(2)}) copy-start(bf16[128]{0:T(256)(128)(2,1)} %param.22) | copy-start | bytes 772
  7.2 21.9 %copy-start.36 = (bf16[128]{0:T(256)(128)(2,1)S(1)}, bf16[128]{0:T(256)(128)(2,1)}, u32[]{:S(2)}) copy-start(bf16[128]{0:T(256)(128)(2,1)} %param.26) | copy-start | bytes 772
  7.3 22.1 %copy-start.37 = (bf16[128]{0:T(256)(128)(2,1)S(1)}, bf16[128]{0:T(256)(128)(2,1)}, u32[]{:S(2)}) copy-start(bf16[128]{0:T(256)(128)(2,1)} %param.19) | copy-start | bytes 772
  7.3 22.3 %copy-start.38 = (bf16[128]{0:T(256)(128)(2,1)S(1)}, bf16[128]{0:T(256)(128)(2,1)}, u32[]{:S(2)}) copy-start(bf16[128]{0:T(256)(128)(2,1)} %param.20) | copy-start | bytes 772
  7.3 22.5 %copy-start.30 = (bf16[512]{0:T(512)(128)(2,1)S(1)}, bf16[512]{0:T(512)(128)(2,1)}, u32[]{:S(2)}) copy-start(bf16[512]{0:T(512)(128)(2,1)} %param.24) | copy-start | bytes 3076
  7.3 43.6 %copy-start.3 = (bf16[1,256,2048]{2,1,0:T(8,128)(2,1)S(1)}, bf16[1,256,2048]{2,1,0:T(8,128)(2,1)}, u32[]{:S(2)}) copy-start(bf16[1,256,2048]{2,1,0:T(8,128)(2,1)} %param.16) | copy-start | bytes 3145732
  7.3 46.4 %all-gather.20.cloned.1.call-start = ((), (), s32[]{:S(2)}) async-start(), calls=%async_computation.16 | async-start | bytes 1310720 | tf_op jit(solution)/shard_map/all_gather | solution.py:189
  9.0 97.5 %all-gather.18.cloned.1.call-start = ((), (), s32[]{:S(2)}) async-start(), calls=%async_computation.15 | async-start | bytes 3932160 | tf_op jit(solution)/shard_map/all_gather | solution.py:136
  28.0 134.0 %all-gather.16.cloned.1.call-start = ((), (), s32[]{:S(2)}) async-start(), calls=%async_computation.14 | async-start | bytes 9437184 | tf_op jit(solution)/shard_map/all_gather | solution.py:42
  53.6 228.7 %all-gather.22.cloned.1.call-start = ((), (), s32[]{:S(2)}) async-start(), calls=%async_computation.17 | async-start | bytes 9437184 | tf_op jit(solution)/shard_map/all_gather | solution.py:42
  61.3 23.3 %all-to-all-start.2 = ((bf16[4,128,1024]{1,2,0:T(8,128)(2,1)}), bf16[4,128,1024]{1,2,0:T(8,128)(2,1)}, u32[]{:S(2)}, u32[]{:S(2)}) async-start(bf16[4,128,1024]{1,2,0:T(8,128)(2,1)} %bitcast.20), calls=%async_computation.2 | async-start | bytes 2097152 | tf_op jit(solution)/shard_map/all_to_all | solution.py:135
  65.6 360.7 %all-gather.26.cloned.1.call-start = ((), (), s32[]{:S(2)}) async-start(), calls=%async_computation.19 | async-start | bytes 5242880 | tf_op jit(solution)/shard_map/all_gather | solution.py:136
  86.9 339.4 %all-gather.24.cloned.1.call-start = ((), (), s32[]{:S(2)}) async-start(), calls=%async_computation.18 | async-start | bytes 9437184 | tf_op jit(solution)/shard_map/all_gather | solution.py:42
  291.5 150.7 %all-gather.30.cloned.1.call-start = ((), (), s32[]{:S(2)}) async-start(), calls=%async_computation.29 | async-start | bytes 9437184 | tf_op jit(solution)/shard_map/all_gather | solution.py:42
  292.2 251.3 %reduce-scatter.11.cloned.1.call-start = ((), (), s32[]{:S(2)}) async-start(), calls=%async_computation.21 | async-start | bytes 9437184 | tf_op jit(solution)/shard_map/reduce_scatter | solution.py:46
  294.7 27.2 %copy-start.9 = (bf16[256,2048]{1,0:T(8,128)(2,1)}, bf16[256,2048]{1,0:T(8,128)(2,1)S(1)}, u32[]{:S(2)}) copy-start(bf16[256,2048]{1,0:T(8,128)(2,1)S(1)} %get-tuple-element.71) | copy-start | bytes 3145732
  294.7 27.2 %collective-permute-start = (bf16[256,2048]{1,0:T(8,128)(2,1)S(1)}, bf16[256,2048]{1,0:T(8,128)(2,1)S(1)}, u32[]{:S(2)}, u32[]{:S(2)}) collective-permute-start(bf16[256,2048]{1,0:T(8,128)(2,1)S(1)} %get-tuple-element.71), channel_id=1, source_target_pairs={{0,12},{4,0},{8,4},{12,8},{1,13},{5,1},{9,5},{13,9},{2,14},{6,2},{... | collective-permute-start | bytes 3145736 | tf_op jit(solution)/shard_map/ppermute | solution.py:197
  323.6 92.9 %collective-permute-start.1 = (bf16[512,2048]{1,0:T(8,128)(2,1)}, bf16[512,2048]{1,0:T(8,128)(2,1)}, u32[]{:S(2)}, u32[]{:S(2)}) collective-permute-start(bf16[512,2048]{1,0:T(8,128)(2,1)} %pad_maximum_fusion), channel_id=1, source_target_pairs={{0,8},{4,12},{8,0},{12,4},{1,9},{5,13},{9,1},{13,5},{2,10},{6,14},... | collective-permute-start | bytes 6291464 | tf_op jit(solution)/shard_map/ppermute | solution.py:197
  325.7 96.3 %copy-start.11 = (bf16[256,2048]{1,0:T(8,128)(2,1)S(1)}, bf16[256,2048]{1,0:T(8,128)(2,1)}, u32[]{:S(2)}) copy-start(bf16[256,2048]{1,0:T(8,128)(2,1)} %copy-done.10) | copy-start | bytes 3145732
  472.1 146.6 %reduce-scatter.9.cloned.1.call-start = ((), (), s32[]{:S(2)}) async-start(), calls=%async_computation.20 | async-start | bytes 9437184 | tf_op jit(solution)/shard_map/reduce_scatter | solution.py:46
  486.8 131.9 %copy-start.21 = (f32[2048]{0:T(1024)S(1)}, f32[2048]{0:T(1024)}, u32[]{:S(2)}) copy-start(f32[2048]{0:T(1024)} %get-tuple-element.75) | copy-start | bytes 24580
  486.8 357.9 %reduce-scatter.23.cloned.1.call-start = ((), (), s32[]{:S(2)}) async-start(), calls=%async_computation.27 | async-start | bytes 5242880 | tf_op jit(solution)/shard_map/reduce_scatter | solution.py:262
  635.3 18.7 %all-to-all-start.3 = ((bf16[8,256,256]{1,2,0:T(8,128)(2,1)}), bf16[8,256,256]{1,2,0:T(8,128)(2,1)}, u32[]{:S(2)}, u32[]{:S(2)}) async-start(bf16[8,256,256]{1,2,0:T(8,128)(2,1)} %bitcast.208), calls=%async_computation.5 | async-start | bytes 2097152 | tf_op jit(solution)/shard_map/all_to_all | solution.py:50
  639.6 205.8 %reduce-scatter.21.cloned.1.call-start = ((), (), s32[]{:S(2)}) async-start(), calls=%async_computation.26 | async-start | bytes 5242880 | tf_op jit(solution)/shard_map/reduce_scatter | solution.py:139
  653.9 232.0 %reduce-scatter.15.cloned.1.call-start = ((), (), s32[]{:S(2)}) async-start(), calls=%async_computation.23 | async-start | bytes 3932160 | tf_op jit(solution)/shard_map/reduce_scatter | solution.py:139
  659.0 21.4 %copy-start.7 = (bf16[2,1024,4,64]{1,0,3,2:T(2,128)(2,1)S(1)}, bf16[2,1024,4,64]{1,0,3,2:T(2,128)(2,1)}, u32[]{:S(2)}) copy-start(bf16[2,1024,4,64]{1,0,3,2:T(2,128)(2,1)} %reshape_reshape_transpose_reshape_reshape.3) | copy-start | bytes 3145732
  659.1 21.4 %copy-start.13 = (bf16[2,1024,4,64]{1,3,2,0:T(8,128)(2,1)S(1)}, bf16[2,1024,4,64]{1,3,2,0:T(8,128)(2,1)}, u32[]{:S(2)}) copy-start(bf16[2,1024,4,64]{1,3,2,0:T(8,128)(2,1)} %copy.114) | copy-start | bytes 3145732
  824.3 136.4 %reduce-scatter.13.cloned.1.call-start = ((), (), s32[]{:S(2)}) async-start(), calls=%async_computation.22 | async-start | bytes 9437184 | tf_op jit(solution)/shard_map/reduce_scatter | solution.py:46
  836.2 199.5 %reduce-scatter.17.cloned.1.call-start = ((), (), s32[]{:S(2)}) async-start(), calls=%async_computation.24 | async-start | bytes 9437184 | tf_op jit(solution)/shard_map/reduce_scatter | solution.py:46
  844.6 44.8 %copy-start.8 = (bf16[1,256,2048]{2,1,0:T(8,128)(2,1)S(1)}, bf16[1,256,2048]{2,1,0:T(8,128)(2,1)}, u32[]{:S(2)}) copy-start(bf16[1,256,2048]{2,1,0:T(8,128)(2,1)} %param.31) | copy-start | bytes 3145732
  844.6 45.0 %copy-start.29 = (f32[1024]{0:T(1024)S(1)}, f32[1024]{0:T(1024)}, u32[]{:S(2)}) copy-start(f32[1024]{0:T(1024)} %get-tuple-element.99) | copy-start | bytes 12292
  844.6 116.1 %copy-start.4 = (bf16[1,256,2048]{2,1,0:T(8,128)(2,1)S(1)}, bf16[1,256,2048]{2,1,0:T(8,128)(2,1)}, u32[]{:S(2)}) copy-start(bf16[1,256,2048]{2,1,0:T(8,128)(2,1)} %param.16) | copy-start | bytes 3145732
  844.6 116.1 %copy-start.19 = (f32[2048]{0:T(1024)S(1)}, f32[2048]{0:T(1024)}, u32[]{:S(2)}) copy-start(f32[2048]{0:T(1024)} %copy-done.18) | copy-start | bytes 24580
  844.6 116.1 %copy-start.26 = (f32[256]{0:T(256)S(1)}, f32[256]{0:T(256)}, u32[]{:S(2)}) copy-start(f32[256]{0:T(256)} %copy-done.25) | copy-start | bytes 3076
  844.6 116.1 %copy-start.28 = (f32[256]{0:T(256)S(1)}, f32[256]{0:T(256)}, u32[]{:S(2)}) copy-start(f32[256]{0:T(256)} %copy-done.27) | copy-start | bytes 3076
  844.7 118.3 %copy-start.23 = (f32[2048]{0:T(1024)S(1)}, f32[2048]{0:T(1024)}, u32[]{:S(2)}) copy-start(f32[2048]{0:T(1024)} %get-tuple-element.60) | copy-start | bytes 24580
  844.7 118.4 %copy-start.22 = (f32[2048]{0:T(1024)S(1)}, f32[2048]{0:T(1024)}, u32[]{:S(2)}) copy-start(f32[2048]{0:T(1024)} %get-tuple-element.66) | copy-start | bytes 24580
  844.7 118.4 %copy-start.24 = (f32[2048]{0:T(1024)S(1)}, f32[2048]{0:T(1024)}, u32[]{:S(2)}) copy-start(f32[2048]{0:T(1024)} %get-tuple-element.68) | copy-start | bytes 24580
  844.7 191.0 %copy-start.40 = (u32[32]{0:T(128)S(1)}, u32[32]{0:T(128)}, u32[]{:S(2)}) copy-start(u32[32]{0:T(128)} %constant.220) | copy-start | bytes 388
  844.7 225.5 %all-gather.28.cloned.1.call-start = ((), (), s32[]{:S(2)}) async-start(), calls=%async_computation.28 | async-start | bytes 3145728 | tf_op jit(solution)/shard_map/all_gather | solution.py:153
  845.3 259.5 %all-gather.34.cloned.1.call-start = ((), (), s32[]{:S(2)}) async-start(), calls=%async_computation.31 | async-start | bytes 3145728 | tf_op jit(solution)/shard_map/all_gather | solution.py:141
  885.9 15.1 %all-to-all-start.4 = ((bf16[4,128,768]{2,1,0:T(8,128)(2,1)}), bf16[4,128,768]{2,1,0:T(8,128)(2,1)S(1)}, u32[]{:S(2)}, u32[]{:S(2)}) async-start(bf16[4,128,768]{2,1,0:T(8,128)(2,1)} %bitcast.222), calls=%async_computation.8 | async-start | bytes 1572864 | tf_op jit(solution)/shard_map/all_to_all | solution.py:140
  889.4 244.6 %all-gather.32.cloned.1.call-start = ((), (), s32[]{:S(2)}) async-start(), calls=%async_computation.30 | async-start | bytes 2359296 | tf_op jit(solution)/shard_map/all_gather | solution.py:141
  901.9 322.6 %all-reduce.4.cloned.1.call-start = ((), (), s32[]{:S(2)}) async-start(), calls=%async_computation.32 | async-start | bytes 196608
  963.8 289.3 %reduce-scatter.19.cloned.1.call-start = ((), (), s32[]{:S(2)}) async-start(), calls=%async_computation.25 | async-start | bytes 1310720 | tf_op jit(solution)/shard_map/reduce_scatter | solution.py:266
  1136.3 126.6 %copy-start.1 = (bf16[128,2048]{1,0:T(8,128)(2,1)S(1)}, bf16[128,2048]{1,0:T(8,128)(2,1)}, u32[]{:S(2)}) copy-start(bf16[128,2048]{1,0:T(8,128)(2,1)} %param.21) | copy-start | bytes 1572868
  (19 other events, 144.6 us)
Sparse Core Ops, SparseCore 0:
  10.3 31.0 all-gather.19
  43.5 62.9 all-gather.17
  108.9 53.0 all-gather.15
  163.7 54.3 all-gather.21
  220.1 83.0 all-gather.25
  305.6 53.5 all-gather.23
  361.0 54.3 all-gather.29
  472.3 71.2 reduce-scatter.10
  547.4 71.2 reduce-scatter.8
  620.8 76.7 reduce-scatter.22
  700.6 77.2 reduce-scatter.20
  824.4 61.4 reduce-scatter.14
  889.3 71.2 reduce-scatter.12
  964.4 71.2 reduce-scatter.16
  1037.1 33.1 all-gather.27
  1071.6 33.1 all-gather.33
  1106.8 27.1 all-gather.31
  1137.3 87.1 all-reduce.3
  1226.9 26.1 reduce-scatter.18
